TPU v7x, 256 devices: a whole 4x4x8 slice. The times are simulated.
256 devices in a mesh: bubble: 16 (over y_hi, z), panel: 16 (over y_lo, x, core).
Axes of the slice: x: 4, y: 4 (y_hi: 2, y_lo: 2; y = y_hi * 2 + y_lo), z: 8, core: 2. Of those that a mesh axis runs over, the one named last changes fastest.
Arguments:
- density: float32 [128, 12288], P('bubble', 'panel'), may hold values from -6 to 6
- right_side: float32 [128, 12288], P('bubble', 'panel'), may hold values from -6 to 6
- inv_diag: bfloat16 [128, 96, 128, 128], P('bubble', 'panel')
- near_vals: bfloat16 [128, 96, 4, 128, 128], P('bubble', 'panel'), may hold values from -0.25 to 0.25
- near_bubble: int32 [128, 96, 4], P('bubble', 'panel'), may hold values from 0 to 127, as said below
- near_block: int32 [128, 96, 4], P('bubble', 'panel'), may hold values from 0 to 95
- near_count: int32 [128, 96], P('bubble', 'panel'), may hold values from 1 to 4, as said below
- colour: int32 [128], P('bubble'), may hold values from 0 to 1
- moment_map: bfloat16 [128, 16, 12288], P('bubble', None, 'panel'), may hold values from -0.0546875 to 0.0546875
- spread_map: bfloat16 [128, 16, 12288], P('bubble', None, 'panel'), may hold values from -0.125 to 0.125
- centres: float32 [3, 128], replicated, may hold values from 0.2 to 6
Outputs:
- relaxed: float32 [128, 12288], P('bubble', 'panel')
Inputs may be any that keep to these rules, and one draw needn't show every extreme that they name: `near_bubble`: every slot of bubble b names a bubble within 8 of b. `near_count`: the first row block of every bubble uses all 4 slots.
All inputs are finite; a program needn't handle non-finite values.
Results may differ from a plain program's by a relative error of at most 0.0041.
Values may be sent and summed in bfloat16 or wider, within the bound.
No kernel may reach another device: no remote copies, remote signals or barrier semaphores. Data moves between devices by JAX's collectives and lax.ppermute only.
A program may use at most 64 MiB of HBM per device.

v0:
```python
import jax
import jax.numpy as jnp
from jax import lax
from jax.sharding import PartitionSpec as P


def with_halo(shard, sides, width):
    for axis, dim in sides:
        peers, length = (lax.axis_size(axis), shard.shape[dim])
        up = [(i, (i + 1) % peers) for i in range(peers - 1)]
        down = [(j, i) for i, j in up]
        last = lax.slice_in_dim(shard, length - width, length, axis=dim)
        first = lax.slice_in_dim(shard, 0, width, axis=dim)
        before = lax.ppermute(last, axis, up)
        after = lax.ppermute(first, axis, down)
        shard = jnp.concatenate([before, shard, after], axis=dim)
    return shard


def near_field(
    neighbourhood, near_vals, near_bubble, near_block, near_count, first_bubble, block_size
):
    rim_count = neighbourhood.shape[0]
    blocks = neighbourhood.reshape(rim_count, neighbourhood.shape[1] // block_size, block_size)
    local_bubble = near_bubble - first_bubble
    sources = blocks[local_bubble, near_block]
    live_slot = jnp.arange(near_vals.shape[2])[None, None, :] < near_count[:, :, None]
    sources = jnp.where(live_slot[:, :, :, None], sources, jnp.zeros_like(sources))
    return jnp.einsum("brsij,brsj->bri", near_vals, sources, preferred_element_type=jnp.float32)


def far_kernel(centres, my_bubbles, reach):
    centre_mine = centres[:, my_bubbles]
    diff = centre_mine[:, :, None] - centres[:, None, :]
    direct_sq = jnp.sum(diff * diff, axis=0)
    mirrored = centre_mine[2][:, None] + centres[2][None, :]
    image_sq = diff[0] * diff[0] + diff[1] * diff[1] + mirrored * mirrored
    kernel = 1.0 / jnp.sqrt(direct_sq + 1.0) + 1.0 / jnp.sqrt(image_sq + 1.0)
    gap = jnp.abs(my_bubbles[:, None] - jnp.arange(centres.shape[1])[None, :])
    return jnp.where(gap > reach, kernel, jnp.zeros_like(kernel))


def per_device(
    density,
    right_side,
    inv_diag,
    near_vals,
    near_bubble,
    near_block,
    near_count,
    colour,
    moment_map,
    spread_map,
    centres,
):
    bub_dev = density.shape[0]
    panels_dev = density.shape[1]
    block_size = inv_diag.shape[2]
    my_index = lax.axis_index("bubble")
    my_bubbles = my_index * bub_dev + jnp.arange(bub_dev, dtype=jnp.int32)
    first_bubble = my_index * bub_dev - bub_dev
    kernel = far_kernel(centres, my_bubbles, bub_dev)
    relaxed = density
    for colour_now in range(2):
        dens_bf = relaxed.astype(jnp.bfloat16)
        panel_full = lax.all_gather(dens_bf, "panel", axis=1, tiled=True)
        neighbourhood = with_halo(panel_full, (("bubble", 0),), bub_dev)
        near = near_field(
            neighbourhood, near_vals, near_bubble, near_block, near_count, first_bubble, block_size
        )
        partial_value = jnp.einsum(
            "bki,bi->bk", moment_map, dens_bf, preferred_element_type=jnp.float32
        )
        own_moments = lax.psum(partial_value, "panel")
        all_moments = lax.all_gather(own_moments, "bubble", axis=0, tiled=True)
        far_coeff = jnp.dot(kernel, all_moments, precision=lax.Precision.HIGHEST).astype(
            jnp.bfloat16
        )
        far = jnp.einsum("bki,bk->bi", spread_map, far_coeff, preferred_element_type=jnp.float32)
        remainder = (right_side - near.reshape(bub_dev, panels_dev) - far).astype(jnp.bfloat16)
        remainder = remainder.reshape(bub_dev, panels_dev // block_size, block_size)
        updated = jnp.einsum(
            "brij,brj->bri", inv_diag, remainder, preferred_element_type=jnp.float32
        )
        relaxed = jnp.where(
            (colour == colour_now)[:, None], updated.reshape(bub_dev, panels_dev), relaxed
        )
    return relaxed


def solution(mesh):
    in_specs = (
        P("bubble", "panel"),
        P("bubble", "panel"),
        P("bubble", "panel", None, None),
        P("bubble", "panel", None, None, None),
        P("bubble", "panel", None),
        P("bubble", "panel", None),
        P("bubble", "panel"),
        P("bubble"),
        P("bubble", None, "panel"),
        P("bubble", None, "panel"),
        P(),
    )
    out_specs = P("bubble", "panel")
    return jax.shard_map(
        per_device, mesh=mesh, in_specs=in_specs, out_specs=out_specs, check_vma=False
    )
```

profile of v0, /device:TPU:8, one launch (start us, length us, event | category | flops | bytes accessed | tf_op | source)
XLA Modules:
  0.0 209.6 jit_solution(4248419762880765899)
XLA Ops:
  0.0 0.9 convert_element_type.18
  0.9 19.1 %all_gather.12 = bf16[8,12288]{1,0:T(8,128)(2,1)S(1)} all-gather(bf16[8,768]{1,0:T(8,128)(2,1)S(1)} %convert_element_type.18), channel_id=1, replica_groups=mesh['bubble'=16,'panel'=16] {'panel'}, dimensions={1}, use_global_device_ids=true | all-gather | bytes 208896 | tf_op jit(solution)/shard_map/all_gather | solution.py:66
  19.9 3.8 %collective-permute-start = (bf16[8,12288]{1,0:T(8,128)(2,1)S(1)}, bf16[8,12288]{1,0:T(8,128)(2,1)S(1)}, u32[]{:S(2)}, u32[]{:S(2)}) collective-permute-start(bf16[8,12288]{1,0:T(8,128)(2,1)S(1)} %all_gather.12), channel_id=1, source_target_pairs={{0,16},{16,32},{32,48},{48,64},{64,80},{80,96},{96,112},{112,128},... | collective-permute-start | bytes 589832 | tf_op jit(solution)/shard_map/ppermute | solution.py:14
  23.8 1.3 collective-permute-start.1
  25.1 0.8 copy.18
  27.4 0.7 convert_bitcast_fusion
  28.1 0.8 multiply_reduce_fusion
  28.9 1.1 fusion.16
  30.0 27.2 %psum.14 = f32[8,16]{1,0:T(8,128)S(1)} all-reduce(f32[8,16]{1,0:T(8,128)S(1)} %bitcast.107), channel_id=1, replica_groups=mesh['bubble'=16,'panel'=16] {'panel'}, use_global_device_ids=true, to_apply=%region_1.2 | all-reduce | flops 128 | bytes 1024 | tf_op jit(solution)/shard_map/psum | solution.py:74
  57.2 44.4 %all_gather.13 = f32[128,16]{1,0:T(8,128)S(1)} all-gather(f32[8,16]{1,0:T(8,128)S(1)} %psum.14), channel_id=1, replica_groups=mesh['bubble'=16,'panel'=16] {'bubble'}, dimensions={0}, use_global_device_ids=true | all-gather | bytes 8704 | tf_op jit(solution)/shard_map/all_gather | solution.py:75
  101.6 0.7 fusion.22
  102.5 0.8 iota_compare_fusion
  103.5 1.1 fusion.34
  105.5 2.5 %gather_fusion = bf16[192,128]{1,0:T(8,128)(2,1)S(1)} fusion(bf16[24,96,128]{2,1,0:T(8,128)(2,1)S(1)} %bitcast.101, s32[192]{0:T(256)S(1)} %reshape.62), kind=kCustom, calls=%fused_computation | custom fusion | bytes 99840 | tf_op jit(solution)/shard_map/gather | solution.py:26
  108.1 4.5 %fusion.4 = f32[8,6,1,128,1]{3,2,4,1,0:T(1,128)S(1)} fusion(bf16[8,6,4,128,128]{4,3,2,1,0:T(8,128)(2,1)} %param.14, bf16[8,6,4,128,1]{3,2,1,0,4:T(4,128)(2,1)S(1)} %select_bitcast_fusion.1), kind=kOutput, calls=%fused_computation.11 | convolution fusion | flops 6291456 | bytes 6365184 | tf_op jit(solution)/shard_map/brsij,brsj->bri/dot_general | solution.py:29
  112.7 0.9 fusion.14
  113.7 16.5 %all_gather.14 = bf16[8,12288]{1,0:T(8,128)(2,1)S(1)} all-gather(bf16[8,768]{1,0:T(8,128)(2,1)S(1)} %fusion.36), channel_id=1, replica_groups=mesh['bubble'=16,'panel'=16] {'panel'}, dimensions={1}, use_global_device_ids=true | all-gather | bytes 208896 | tf_op jit(solution)/shard_map/all_gather | solution.py:66
  130.2 1.3 collective-permute-start.2
  131.5 1.3 collective-permute-start.3
  132.9 29.1 %psum.15 = f32[8,16]{1,0:T(8,128)S(1)} all-reduce(f32[8,16]{1,0:T(8,128)S(1)} %bitcast.108), channel_id=1, replica_groups=mesh['bubble'=16,'panel'=16] {'panel'}, use_global_device_ids=true, to_apply=%region_2.3 | all-reduce | flops 128 | bytes 1024 | tf_op jit(solution)/shard_map/psum | solution.py:74
  162.0 38.3 %all_gather.15 = f32[128,16]{1,0:T(8,128)S(1)} all-gather(f32[8,16]{1,0:T(8,128)S(1)} %psum.15), channel_id=1, replica_groups=mesh['bubble'=16,'panel'=16] {'bubble'}, dimensions={0}, use_global_device_ids=true | all-gather | bytes 8704 | tf_op jit(solution)/shard_map/all_gather | solution.py:75
  200.8 2.5 %gather_fusion.2 = bf16[192,128]{1,0:T(8,128)(2,1)S(1)} fusion(bf16[24,96,128]{2,1,0:T(8,128)(2,1)S(1)} %bitcast.100, s32[192]{0:T(256)S(1)} %reshape.62), kind=kCustom, calls=%fused_computation.2 | custom fusion | bytes 99840 | tf_op jit(solution)/shard_map/gather | solution.py:26
  203.5 4.5 %fusion.2 = f32[8,6,1,128,1]{3,2,4,1,0:T(1,128)S(1)} fusion(bf16[8,6,4,128,128]{4,3,2,1,0:T(8,128)(2,1)} %param.14, bf16[8,6,4,128,1]{3,2,1,0,4:T(4,128)(2,1)S(1)} %select_bitcast_fusion), kind=kOutput, calls=%fused_computation.9 | convolution fusion | flops 6291456 | bytes 6365184 | tf_op jit(solution)/shard_map/brsij,brsj->bri/dot_general | solution.py:29
  208.0 0.9 fusion.10
  (39 shorter events, 4.5 us)
Async XLA Ops:
  0.0 112.7 %copy-start = (bf16[8,6,128,128]{3,2,1,0:T(8,128)(2,1)S(1)}, bf16[8,6,128,128]{3,2,1,0:T(8,128)(2,1)}, u32[]{:S(2)}) copy-start(bf16[8,6,128,128]{3,2,1,0:T(8,128)(2,1)} %param.13) | copy-start | bytes 4718596
  19.9 85.4 %collective-permute-start = (bf16[8,12288]{1,0:T(8,128)(2,1)S(1)}, bf16[8,12288]{1,0:T(8,128)(2,1)S(1)}, u32[]{:S(2)}, u32[]{:S(2)}) collective-permute-start(bf16[8,12288]{1,0:T(8,128)(2,1)S(1)} %all_gather.12), channel_id=1, source_target_pairs={{0,16},{16,32},{32,48},{48,64},{64,80},{80,96},{96,112},{112,128},... | collective-permute-start | bytes 589832 | tf_op jit(solution)/shard_map/ppermute | solution.py:14
  23.8 81.5 %collective-permute-start.1 = (bf16[8,12288]{1,0:T(8,128)(2,1)S(1)}, bf16[8,12288]{1,0:T(8,128)(2,1)S(1)}, u32[]{:S(2)}, u32[]{:S(2)}) collective-permute-start(bf16[8,12288]{1,0:T(8,128)(2,1)S(1)} %all_gather.12), channel_id=1, source_target_pairs={{16,0},{32,16},{48,32},{64,48},{80,64},{96,80},{112,96},{128,112},... | collective-permute-start | bytes 589832 | tf_op jit(solution)/shard_map/ppermute | solution.py:15
  108.1 4.5 %copy-start.3 = (f32[8,768]{1,0:T(8,128)S(1)}, f32[8,768]{1,0:T(8,128)}, u32[]{:S(2)}) copy-start(f32[8,768]{1,0:T(8,128)} %param.12) | copy-start | bytes 73732
  112.6 1.0 copy-start.2
  112.6 20.1 %copy-start.4 = (bf16[8,16,768]{2,1,0:T(8,128)(2,1)S(1)}, bf16[8,16,768]{2,1,0:T(8,128)(2,1)}, u32[]{:S(2)}) copy-start(bf16[8,16,768]{2,1,0:T(8,128)(2,1)} %param.19) | copy-start | bytes 589828
  112.6 87.8 %copy-start.1 = (bf16[8,16,768]{2,1,0:T(8,128)(2,1)S(1)}, bf16[8,16,768]{2,1,0:T(8,128)(2,1)}, u32[]{:S(2)}) copy-start(bf16[8,16,768]{2,1,0:T(8,128)(2,1)} %param.20) | copy-start | bytes 589828
  130.2 70.5 %collective-permute-start.2 = (bf16[8,12288]{1,0:T(8,128)(2,1)S(1)}, bf16[8,12288]{1,0:T(8,128)(2,1)S(1)}, u32[]{:S(2)}, u32[]{:S(2)}) collective-permute-start(bf16[8,12288]{1,0:T(8,128)(2,1)S(1)} %all_gather.14), channel_id=1, source_target_pairs={{0,16},{16,32},{32,48},{48,64},{64,80},{80,96},{96,112},{112,128},... | collective-permute-start | bytes 589832 | tf_op jit(solution)/shard_map/ppermute | solution.py:14
  131.5 69.2 %collective-permute-start.3 = (bf16[8,12288]{1,0:T(8,128)(2,1)S(1)}, bf16[8,12288]{1,0:T(8,128)(2,1)S(1)}, u32[]{:S(2)}, u32[]{:S(2)}) collective-permute-start(bf16[8,12288]{1,0:T(8,128)(2,1)S(1)} %all_gather.14), channel_id=1, source_target_pairs={{16,0},{32,16},{48,32},{64,48},{80,64},{96,80},{112,96},{128,112},... | collective-permute-start | bytes 589832 | tf_op jit(solution)/shard_map/ppermute | solution.py:15
where the time goes:
time: 214 us; the launch traced here: 210 us
  blocking collectives  175 us (82%)
  matrix products  13.6 us (6%)
  local copies, waits for them, and re-layouts  7.75 us (4%)
  starting transfers between devices  7.69 us (4%)
  other arithmetic  5.75 us (3%)
    all_gather x2, blocking collectives, per_device(): all_moments = lax.all_gather(own_moments, 'bubble', axis=0, tiled=True)  82.7 us
    psum x2, blocking collectives, per_device(): own_moments = lax.psum(partial_value, 'panel')  56.3 us
    all_gather x2, blocking collectives, per_device(): panel_full = lax.all_gather(dens_bf, 'panel', axis=1, tiled=True)  35.6 us
    dot_general x2, matrix products, near_field(): jnp.einsum('brsij,brsj->bri', near_vals, sources, preferred_element_type=...  9.02 us
    ppermute x2, starting transfers between devices, with_halo(): before = lax.ppermute(last, axis, up)  5.11 us
    gather x2, local copies, waits for them, and re-layouts, near_field(): sources = blocks[local_bubble, near_block]  5.03 us
  transfers between devices with their start and end apart: 4, of which 0 were waited for; matrix products, arithmetic and copies ran while one was open for 4% of the time, Pallas kernels for 0%

commit v1 on v0

v1 whole, which is shorter than its diff:
```python
import functools

import jax
import jax.numpy as jnp
from jax import lax
from jax.experimental import pallas as pl
from jax.experimental.pallas import tpu as pltpu
from jax.sharding import PartitionSpec as P

NT = (((1,), (1,)), ((), ()))
NN = (((1,), (0,)), ((), ()))


def row_ids(shape):
    return lax.broadcasted_iota(jnp.int32, shape, 0)


def emit_message(tiles, moment_map, message):
    bub, lanes = tiles[0].shape
    peers, slots = message.shape[:2]
    k = lanes // bub
    dens = jnp.concatenate(tiles, axis=1).astype(jnp.bfloat16)
    cross = lax.dot_general(dens, moment_map[...], NT, preferred_element_type=jnp.float32)
    rows = row_ids((bub, lanes))
    own = lax.broadcasted_iota(jnp.int32, (bub, lanes), 1) // k == rows
    share = jnp.sum(jnp.where(own, cross, 0.0), axis=0, keepdims=True)
    top = share.astype(jnp.bfloat16).astype(jnp.float32)
    rest = share - top
    mid = rest.astype(jnp.bfloat16).astype(jnp.float32)
    low = rest - mid
    parts = jnp.where(
        rows == 0, top, jnp.where(rows == 1, mid, jnp.where(rows == 2, low, 0.0))
    ).astype(jnp.bfloat16)
    blocks = [t.astype(jnp.bfloat16) for t in tiles] + [parts]
    for p in range(peers):
        for j in range(slots):
            message[p, j] = blocks[j]


def first_kernel(density, moment_map, message):
    n = message.shape[1] - 1
    w = message.shape[3]
    tiles = [density[:, j * w : (j + 1) * w] for j in range(n)]
    emit_message(tiles, moment_map, message)


def moment_kernel(received, out):
    peers, slots = received.shape[:2]
    total = received[0, slots - 1].astype(jnp.float32)
    for p in range(1, peers):
        total = total + received[p, slots - 1].astype(jnp.float32)
    row = jnp.sum(total, axis=0, keepdims=True)
    for g in range(out.shape[0]):
        out[g] = row


def sweep_kernel(
    colour_now,
    last,
    index,
    colour,
    before,
    own,
    after,
    moments,
    far_weight,
    spread_map,
    right_side,
    relaxed,
    moment_map,
    near_vals,
    inv_diag,
    *refs,
):
    if last:
        out, sources, vals, invs, acc, sem_v, sem_i = refs
    else:
        out, message, sources, vals, invs, acc, sem_v, sem_i = refs
    bub, nblk, slots, blk, _ = near_vals.shape
    peers = own.shape[0]
    k = blk // bub

    def copy_v(b):
        return pltpu.make_async_copy(near_vals.at[b], vals.at[b], sem_v.at[b])

    def copy_i(b):
        return pltpu.make_async_copy(inv_diag.at[b], invs.at[b], sem_i.at[b])

    for b in range(bub):

        @pl.when(colour[b] == colour_now)
        def _():
            copy_v(b).start()

    for b in range(bub):

        @pl.when(colour[b] == colour_now)
        def _():
            copy_i(b).start()

    rows = row_ids((bub, blk))
    for o, ref in enumerate((before, own, after)):
        for p in range(peers):
            for j in range(nblk):
                at = ((o * peers + p) * nblk + j) * bub
                sources[at : at + bub, :] = ref[p, j].astype(jnp.float32)
    sources[3 * peers * nblk * bub :, :] = jnp.zeros((bub, blk), jnp.float32)
    acc[...] = jnp.zeros_like(acc)

    g = far_weight[0] * moments[0]
    for q in range(1, moments.shape[0]):
        g = g + far_weight[q] * moments[q]
    shift = blk // 2
    while shift >= k:
        g = g + pltpu.roll(g, shift, 1)
        shift //= 2
    mine = lax.broadcasted_iota(jnp.int32, (bub, blk), 1) // k == rows
    coeff = jnp.where(mine, g, 0.0).astype(jnp.bfloat16)
    far = lax.dot_general(coeff, spread_map[...], NN, preferred_element_type=jnp.float32)

    def near_of(b, carry):
        @pl.when(colour[b] == colour_now)
        def _():
            copy_v(b).wait()
            here = rows == b
            for r in range(nblk):
                total = acc[r]
                for s in range(slots):
                    i = index[(b * nblk + r) * slots + s]
                    src = jnp.where(here, sources[pl.ds(i, 1), :], 0.0).astype(jnp.bfloat16)
                    total = total + lax.dot_general(
                        src, vals[b, r, s], NT, preferred_element_type=jnp.float32
                    )
                acc[r] = total

        return carry

    lax.fori_loop(0, bub, near_of, 0)
    for r in range(nblk):
        cols = slice(r * blk, (r + 1) * blk)
        acc[r] = right_side[:, cols] - acc[r] - far[:, cols]
        out[:, cols] = jnp.zeros((bub, blk), jnp.float32)

    def solve(b, carry):
        @pl.when(colour[b] == colour_now)
        def _():
            copy_i(b).wait()
            here = rows == b
            for r in range(nblk):
                cols = slice(r * blk, (r + 1) * blk)
                rest = jnp.where(here, acc[r], 0.0).astype(jnp.bfloat16)
                out[:, cols] += lax.dot_general(
                    rest, invs[b, r], NT, preferred_element_type=jnp.float32
                )

        return carry

    lax.fori_loop(0, bub, solve, 0)
    colours = jnp.zeros((bub, blk), jnp.int32)
    for b in range(bub):
        colours = jnp.where(rows == b, colour[b], colours)
    live = colours == colour_now
    tiles = []
    for r in range(nblk):
        cols = slice(r * blk, (r + 1) * blk)
        tile = jnp.where(live, out[:, cols], relaxed[:, cols])
        out[:, cols] = tile
        tiles.append(tile)
    if not last:
        emit_message(tiles, moment_map, message)


def far_weights(centres, my_bubbles, reach, k):
    n_bub, total = my_bubbles.shape[0], centres.shape[1]
    groups = total // n_bub
    theirs = jnp.repeat(centres, k, axis=1).reshape(3, groups, 1, n_bub * k)
    mine = centres[:, my_bubbles].reshape(3, 1, n_bub, 1)
    diff = mine - theirs
    direct_sq = diff[0] * diff[0] + diff[1] * diff[1] + diff[2] * diff[2]
    mirrored = mine[2] + theirs[2]
    image_sq = diff[0] * diff[0] + diff[1] * diff[1] + mirrored * mirrored
    kernel = 1.0 / jnp.sqrt(direct_sq + 1.0) + 1.0 / jnp.sqrt(image_sq + 1.0)
    lane = lax.broadcasted_iota(jnp.int32, kernel.shape, 2)
    q = lax.broadcasted_iota(jnp.int32, kernel.shape, 0) * n_bub + lane // k
    gap = jnp.abs(my_bubbles.reshape(1, n_bub, 1) - q)
    return jnp.where(gap > reach, kernel, jnp.zeros_like(kernel))


VMEM = pl.BlockSpec(memory_space=pltpu.VMEM)
SMEM = pl.BlockSpec(memory_space=pltpu.SMEM)
ANY = pl.BlockSpec(memory_space=pl.ANY)


def per_device(
    density,
    right_side,
    inv_diag,
    near_vals,
    near_bubble,
    near_block,
    near_count,
    colour,
    moment_map,
    spread_map,
    centres,
):
    bub, nblk, slots, blk, _ = near_vals.shape
    k = moment_map.shape[1]
    panels = nblk * blk
    peers, groups = lax.axis_size("panel"), lax.axis_size("bubble")
    my_index = lax.axis_index("bubble")
    my_bubbles = my_index * bub + jnp.arange(bub, dtype=jnp.int32)
    far_weight = far_weights(centres, my_bubbles, bub, k)
    moment_map = moment_map.reshape(bub * k, panels)
    spread_map = spread_map.reshape(bub * k, panels)

    local = near_bubble - (my_index * bub - bub)
    row = ((local // bub) * peers * nblk + near_block) * bub + local % bub
    live = jnp.arange(slots)[None, None, :] < near_count[:, :, None]
    index = jnp.where(live, row, 3 * peers * nblk * bub).reshape(-1)

    message_shape = jax.ShapeDtypeStruct((peers, nblk + 1, bub, blk), jnp.bfloat16)
    relaxed_shape = jax.ShapeDtypeStruct((bub, panels), jnp.float32)
    up = [(i, (i + 1) % groups) for i in range(groups)]
    down = [(j, i) for i, j in up]

    message = pl.pallas_call(
        first_kernel, out_shape=message_shape, in_specs=[VMEM, VMEM], out_specs=VMEM, name="first"
    )(density, moment_map)
    relaxed = density
    for colour_now in range(2):
        last = colour_now == 1
        received = lax.all_to_all(message, "panel", 0, 0, tiled=True)
        before = lax.ppermute(received, "bubble", up)
        after = lax.ppermute(received, "bubble", down)
        own_moments = pl.pallas_call(
            moment_kernel,
            out_shape=jax.ShapeDtypeStruct((groups, 1, blk), jnp.float32),
            in_specs=[VMEM],
            out_specs=VMEM,
            name="moments",
        )(received)
        moments = lax.all_to_all(own_moments, "bubble", 0, 0, tiled=True)
        outs = pl.pallas_call(
            functools.partial(sweep_kernel, colour_now, last),
            out_shape=[relaxed_shape] if last else [relaxed_shape, message_shape],
            in_specs=[SMEM, SMEM] + [VMEM] * 9 + [ANY, ANY],
            out_specs=[VMEM] if last else [VMEM, VMEM],
            scratch_shapes=[
                pltpu.VMEM(((3 * peers * nblk + 1) * bub, blk), jnp.float32),
                pltpu.VMEM((bub, nblk, slots, blk, blk), jnp.bfloat16),
                pltpu.VMEM((bub, nblk, blk, blk), jnp.bfloat16),
                pltpu.VMEM((nblk, bub, blk), jnp.float32),
                pltpu.SemaphoreType.DMA((bub,)),
                pltpu.SemaphoreType.DMA((bub,)),
            ],
            name=f"sweep{colour_now}",
        )(
            index,
            colour,
            before,
            received,
            after,
            moments,
            far_weight,
            spread_map,
            right_side,
            relaxed,
            moment_map,
            near_vals,
            inv_diag,
        )
        if last:
            (relaxed,) = outs
        else:
            relaxed, message = outs
    return relaxed


def solution(mesh):
    in_specs = (
        P("bubble", "panel"),
        P("bubble", "panel"),
        P("bubble", "panel", None, None),
        P("bubble", "panel", None, None, None),
        P("bubble", "panel", None),
        P("bubble", "panel", None),
        P("bubble", "panel"),
        P("bubble"),
        P("bubble", None, "panel"),
        P("bubble", None, "panel"),
        P(),
    )
    out_specs = P("bubble", "panel")
    return jax.shard_map(
        per_device, mesh=mesh, in_specs=in_specs, out_specs=out_specs, check_vma=False
    )
```

time: 214 us -> 88.9 us (0.42); the launches traced: 210 us -> 87.9 us
  blocking collectives: 175 us -> 27 us
  Pallas kernels: 0 us -> 17.8 us
  starting transfers between devices: 7.69 us -> 24 us
  matrix products: 13.6 us -> 0 us
  waiting for transfers between devices: 0.01 us -> 10.9 us
  other arithmetic: 5.75 us -> 1.59 us
    all_gather x4 -> x0, blocking collectives: 118 us -> none  [the longest x2 82.7 us: per_device(): all_moments = lax.all_gather(own_moments, 'bubble', axis=0, tiled=True)]
    psum x2 -> x0, blocking collectives: 56.3 us -> none  [per_device(): own_moments = lax.psum(partial_value, 'panel')]
    all_to_all x0 -> x2, blocking collectives: none -> 27 us  [the longest x1 15.4 us: per_device(): moments = lax.all_to_all(own_moments, 'bubble', 0, 0, tiled=True)]
    pallas_call x0 -> x5, Pallas kernels: none -> 17.8 us  [the longest x2 12.9 us: per_device(): pl.pallas_call(functools.partial(sweep_kernel, colour_now, last), out_sha...]
    dot_general x10 -> x0, matrix products: 13.6 us -> none  [the longest x2 9.02 us: near_field(): jnp.einsum('brsij,brsj->bri', near_vals, sources, preferred_element_type=...]
    all_to_all x0 -> x2, starting transfers between devices: none -> 12.8 us  [the longest x1 7.02 us: per_device(): moments = lax.all_to_all(own_moments, 'bubble', 0, 0, tiled=True)]
    all_to_all x0 -> x2, waiting for transfers between devices: none -> 10.9 us  [the longest x1 8.38 us: per_device(): moments = lax.all_to_all(own_moments, 'bubble', 0, 0, tiled=True)]
    gather x4 -> x2, local copies, waits for them, and re-layouts: 5.66 us -> 0.64 us  [far_weights(): mine = centres[:, my_bubbles].reshape(3, 1, n_bub, 1)]
  transfers between devices with their start and end apart: 4 -> 6, of which waited for: 0 -> 2; matrix products, arithmetic and copies ran while one was open for 4% -> 8% of each run, Pallas kernels for 0% -> 4%
where the time goes in v1:
time: 88.9 us; the launch traced here: 87.9 us
  blocking collectives  27 us (30%)
  starting transfers between devices  24 us (27%)
  Pallas kernels  17.8 us (20%)
  waiting for transfers between devices  10.9 us (12%)
  local copies, waits for them, and re-layouts  6.51 us (7%)
  other arithmetic  1.59 us (2%)
    all_to_all x1, blocking collectives, per_device(): moments = lax.all_to_all(own_moments, 'bubble', 0, 0, tiled=True)  15.4 us
    pallas_call x2, Pallas kernels, per_device(): pl.pallas_call(functools.partial(sweep_kernel, colour_now, last), out_sha...  12.9 us
    all_to_all x1, blocking collectives, per_device(): received = lax.all_to_all(message, 'panel', 0, 0, tiled=True)  11.6 us
    ppermute x2, starting transfers between devices, per_device(): after = lax.ppermute(received, 'bubble', down)  9.09 us
    all_to_all x1, waiting for transfers between devices, per_device(): moments = lax.all_to_all(own_moments, 'bubble', 0, 0, tiled=True)  8.38 us
    all_to_all x1, starting transfers between devices, per_device(): moments = lax.all_to_all(own_moments, 'bubble', 0, 0, tiled=True)  7.02 us
    all_to_all x1, starting transfers between devices, per_device(): received = lax.all_to_all(message, 'panel', 0, 0, tiled=True)  5.78 us
    pallas_call x2, Pallas kernels, per_device(): pl.pallas_call(moment_kernel, out_shape=jax.ShapeDtypeStruct((groups, 1,...  3.13 us
  transfers between devices with their start and end apart: 6, of which 2 were waited for; matrix products, arithmetic and copies ran while one was open for 8% of the time, Pallas kernels for 4%

profile of v1, /device:TPU:8, one launch (start us, length us, event | category | flops | bytes accessed | tf_op | source)
XLA Modules:
  0.0 87.9 jit_solution(3624992318232611845)
XLA Ops:
  0.0 1.8 %first.1 = bf16[16,7,8,128]{3,2,1,0:T(8,128)(2,1)} custom-call(f32[8,768]{1,0:T(8,128)} %relaxed.1, bf16[128,768]{1,0:T(8,128)(2,1)} %bitcast.21), custom_call_target="tpu_custom_call" | custom-call | tf_op jit(solution)/shard_map/first/pallas_call | solution.py:227
  1.8 5.8 %all-to-all-start = ((bf16[16,7,8,128]{3,2,1,0:T(8,128)(2,1)}), bf16[16,7,8,128]{3,2,1,0:T(8,128)(2,1)S(1)}, u32[]{:S(2)}, u32[]{:S(2)}) async-start(bf16[16,7,8,128]{3,2,1,0:T(8,128)(2,1)} %first.1), calls=%async_computation | async-start | bytes 458752 | tf_op jit(solution)/shard_map/all_to_all | solution.py:233
  7.7 0.7 slice_reduce_fusion.1
  8.4 0.8 copy.17
  9.2 0.6 gather_fusion
  10.2 0.8 broadcast_in_dim.20
  11.3 2.5 %all-to-all-done.received.own = bf16[16,7,8,128]{3,2,1,0:T(8,128)(2,1)S(1)} async-done(((bf16[16,7,8,128]{3,2,1,0:T(8,128)(2,1)}), bf16[16,7,8,128]{3,2,1,0:T(8,128)(2,1)S(1)}, u32[]{:S(2)}, u32[]{:S(2)}) %all-to-all-start) | async-done | bytes 229408 | tf_op jit(solution)/shard_map/all_to_all | solution.py:233
  13.8 7.6 %collective-permute-start.1 = (bf16[16,7,8,128]{3,2,1,0:T(8,128)(2,1)S(1)}, bf16[16,7,8,128]{3,2,1,0:T(8,128)(2,1)S(1)}, u32[]{:S(2)}, u32[]{:S(2)}) collective-permute-start(bf16[16,7,8,128]{3,2,1,0:T(8,128)(2,1)S(1)} %all-to-all-done.received.own), channel_id=1, source_target_pairs={{16,0},{32,16},{48,32},{64,48},{80,64},{96,80},{112,96},{128,112},... | collective-permute-start | bytes 688136 | tf_op jit(solution)/shard_map/ppermute | solution.py:235
  21.4 0.7 fusion.5.far_weight
  22.1 0.8 copy.15
  22.8 1.6 %moments.2 = f32[16,1,128]{2,1,0:T(1,128)} custom-call(bf16[16,7,8,128]{3,2,1,0:T(8,128)(2,1)} %copy-done), custom_call_target="tpu_custom_call" | custom-call | tf_op jit(solution)/shard_map/moments/pallas_call | solution.py:236
  24.4 7.0 %all-to-all-start.1 = ((f32[16,1,128]{2,1,0:T(1,128)}), f32[16,1,128]{2,1,0:T(1,128)S(1)}, u32[]{:S(2)}, u32[]{:S(2)}) async-start(f32[16,1,128]{2,1,0:T(1,128)} %moments.2), calls=%async_computation.1 | async-start | bytes 16384 | tf_op jit(solution)/shard_map/all_to_all | solution.py:243
  31.4 0.8 fusion.12
  32.3 0.6 reshape.49.index
  33.0 8.4 %all-to-all-done.1.moments = f32[16,1,128]{2,1,0:T(1,128)S(1)} async-done(((f32[16,1,128]{2,1,0:T(1,128)}), f32[16,1,128]{2,1,0:T(1,128)S(1)}, u32[]{:S(2)}, u32[]{:S(2)}) %all-to-all-start.1) | async-done | bytes 8224 | tf_op jit(solution)/shard_map/all_to_all | solution.py:243
  41.4 0.6 copy-done.6
  42.1 5.1 %sweep0.1 = (f32[8,768]{1,0:T(8,128)}, bf16[16,7,8,128]{3,2,1,0:T(8,128)(2,1)}) custom-call(s32[192]{0:T(256)} %reshape.49.index, s32[8]{0:T(128)} %colour.3, bf16[16,7,8,128]{3,2,1,0:T(8,128)(2,1)} %copy-done.3, bf16[16,7,8,128]{3,2,1,0:T(8,128)(2,1)} %copy-done, bf16[16,7,8,128]{3,2,1,0:T(8,128)(2,1)} %copy-done.2, f32[16,1,128]{2,1,0:T(1,128)} %copy-done.6, ...), custom_call_target="tpu_custom_call" | custom-call | tf_op jit(solution)/shard_map/sweep0/pallas_call | solution.py:244
  47.2 11.6 %all_to_all.20.received.own = bf16[16,7,8,128]{3,2,1,0:T(8,128)(2,1)S(1)} all-to-all(bf16[16,7,8,128]{3,2,1,0:T(8,128)(2,1)} %get-tuple-element.7), channel_id=1, replica_groups=mesh['bubble'=16,'panel'=16] {'panel'}, dimensions={0} | all-to-all | bytes 458752 | tf_op jit(solution)/shard_map/all_to_all | solution.py:233
  58.7 1.5 %collective-permute-start.3 = (bf16[16,7,8,128]{3,2,1,0:T(8,128)(2,1)S(1)}, bf16[16,7,8,128]{3,2,1,0:T(8,128)(2,1)S(1)}, u32[]{:S(2)}, u32[]{:S(2)}) collective-permute-start(bf16[16,7,8,128]{3,2,1,0:T(8,128)(2,1)S(1)} %all_to_all.20.received.own), channel_id=1, source_target_pairs={{16,0},{32,16},{48,32},{64,48},{80,64},{96,80},{112,96},{128,112},... | collective-permute-start | bytes 688136 | tf_op jit(solution)/shard_map/ppermute | solution.py:235
  60.3 2.1 %collective-permute-start.2 = (bf16[16,7,8,128]{3,2,1,0:T(8,128)(2,1)S(1)}, bf16[16,7,8,128]{3,2,1,0:T(8,128)(2,1)S(1)}, u32[]{:S(2)}, u32[]{:S(2)}) collective-permute-start(bf16[16,7,8,128]{3,2,1,0:T(8,128)(2,1)S(1)} %all_to_all.20.received.own), channel_id=1, source_target_pairs={{0,16},{16,32},{32,48},{48,64},{64,80},{80,96},{96,112},{112,128},... | collective-permute-start | bytes 688136 | tf_op jit(solution)/shard_map/ppermute | solution.py:234
  62.3 1.6 %moments.3 = f32[16,1,128]{2,1,0:T(1,128)} custom-call(bf16[16,7,8,128]{3,2,1,0:T(8,128)(2,1)} %copy-done.1), custom_call_target="tpu_custom_call" | custom-call | tf_op jit(solution)/shard_map/moments/pallas_call | solution.py:236
  63.9 15.4 %all_to_all.21.moments = f32[16,1,128]{2,1,0:T(1,128)} all-to-all(f32[16,1,128]{2,1,0:T(1,128)} %moments.3), channel_id=1, replica_groups=mesh['bubble'=16,'panel'=16] {'bubble'}, dimensions={0} | all-to-all | bytes 16384 | tf_op jit(solution)/shard_map/all_to_all | solution.py:243
  79.3 0.7 copy-done.4
  80.1 7.8 %sweep1.1 = f32[8,768]{1,0:T(8,128)} custom-call(s32[192]{0:T(256)} %reshape.49.index, s32[8]{0:T(128)} %colour.3, bf16[16,7,8,128]{3,2,1,0:T(8,128)(2,1)} %copy-done.5, bf16[16,7,8,128]{3,2,1,0:T(8,128)(2,1)} %copy-done.1, bf16[16,7,8,128]{3,2,1,0:T(8,128)(2,1)} %copy-done.4, f32[16,1,128]{2,1,0:T(1,128)} %all_to_all.21.moments, ...), custom_call_target="tpu_custom_call" | custom-call | tf_op jit(solution)/shard_map/sweep1/pallas_call | solution.py:244
  (31 shorter events, 1.2 us)
Async XLA Ops:
  1.8 11.9 %all-to-all-start = ((bf16[16,7,8,128]{3,2,1,0:T(8,128)(2,1)}), bf16[16,7,8,128]{3,2,1,0:T(8,128)(2,1)S(1)}, u32[]{:S(2)}, u32[]{:S(2)}) async-start(bf16[16,7,8,128]{3,2,1,0:T(8,128)(2,1)} %first.1), calls=%async_computation | async-start | bytes 458752 | tf_op jit(solution)/shard_map/all_to_all | solution.py:233
  13.8 9.1 %copy-start = (bf16[16,7,8,128]{3,2,1,0:T(8,128)(2,1)}, bf16[16,7,8,128]{3,2,1,0:T(8,128)(2,1)S(1)}, u32[]{:S(2)}) copy-start(bf16[16,7,8,128]{3,2,1,0:T(8,128)(2,1)S(1)} %all-to-all-done.received.own) | copy-start | bytes 688132
  13.8 27.6 %collective-permute-start.1 = (bf16[16,7,8,128]{3,2,1,0:T(8,128)(2,1)S(1)}, bf16[16,7,8,128]{3,2,1,0:T(8,128)(2,1)S(1)}, u32[]{:S(2)}, u32[]{:S(2)}) collective-permute-start(bf16[16,7,8,128]{3,2,1,0:T(8,128)(2,1)S(1)} %all-to-all-done.received.own), channel_id=1, source_target_pairs={{16,0},{32,16},{48,32},{64,48},{80,64},{96,80},{112,96},{128,112},... | collective-permute-start | bytes 688136 | tf_op jit(solution)/shard_map/ppermute | solution.py:235
  21.3 20.0 %collective-permute-start = (bf16[16,7,8,128]{3,2,1,0:T(8,128)(2,1)S(1)}, bf16[16,7,8,128]{3,2,1,0:T(8,128)(2,1)S(1)}, u32[]{:S(2)}, u32[]{:S(2)}) collective-permute-start(bf16[16,7,8,128]{3,2,1,0:T(8,128)(2,1)S(1)} %all-to-all-done.received.own), channel_id=1, source_target_pairs={{0,16},{16,32},{32,48},{48,64},{64,80},{80,96},{96,112},{112,128},... | collective-permute-start | bytes 688136 | tf_op jit(solution)/shard_map/ppermute | solution.py:234
  24.4 16.9 %all-to-all-start.1 = ((f32[16,1,128]{2,1,0:T(1,128)}), f32[16,1,128]{2,1,0:T(1,128)S(1)}, u32[]{:S(2)}, u32[]{:S(2)}) async-start(f32[16,1,128]{2,1,0:T(1,128)} %moments.2), calls=%async_computation.1 | async-start | bytes 16384 | tf_op jit(solution)/shard_map/all_to_all | solution.py:243
  41.3 0.6 copy-start.6
  41.3 0.7 copy-start.2
  41.4 0.8 copy-start.3
  58.7 3.6 %copy-start.1 = (bf16[16,7,8,128]{3,2,1,0:T(8,128)(2,1)}, bf16[16,7,8,128]{3,2,1,0:T(8,128)(2,1)S(1)}, u32[]{:S(2)}) copy-start(bf16[16,7,8,128]{3,2,1,0:T(8,128)(2,1)S(1)} %all_to_all.20.received.own) | copy-start | bytes 688132
  58.7 20.6 %collective-permute-start.3 = (bf16[16,7,8,128]{3,2,1,0:T(8,128)(2,1)S(1)}, bf16[16,7,8,128]{3,2,1,0:T(8,128)(2,1)S(1)}, u32[]{:S(2)}, u32[]{:S(2)}) collective-permute-start(bf16[16,7,8,128]{3,2,1,0:T(8,128)(2,1)S(1)} %all_to_all.20.received.own), channel_id=1, source_target_pairs={{16,0},{32,16},{48,32},{64,48},{80,64},{96,80},{112,96},{128,112},... | collective-permute-start | bytes 688136 | tf_op jit(solution)/shard_map/ppermute | solution.py:235
  60.3 19.1 %collective-permute-start.2 = (bf16[16,7,8,128]{3,2,1,0:T(8,128)(2,1)S(1)}, bf16[16,7,8,128]{3,2,1,0:T(8,128)(2,1)S(1)}, u32[]{:S(2)}, u32[]{:S(2)}) collective-permute-start(bf16[16,7,8,128]{3,2,1,0:T(8,128)(2,1)S(1)} %all_to_all.20.received.own), channel_id=1, source_target_pairs={{0,16},{16,32},{32,48},{48,64},{64,80},{80,96},{96,112},{112,128},... | collective-permute-start | bytes 688136 | tf_op jit(solution)/shard_map/ppermute | solution.py:234
  79.3 0.7 copy-start.4
  79.3 0.8 copy-start.5

commit v2 on v1

--- a/solution.py
+++ b/solution.py
@@ -54,16 +54,37 @@
         out[g] = row
 
 
+def shift_of(power):
+    assert power & (power - 1) == 0
+    return power.bit_length() - 1
+
+
+def far_weights(centres, first, reach):
+    shape = (reach, centres.shape[1])
+    rows = row_ids(shape)
+    q = lax.broadcasted_iota(jnp.int32, shape, 1)
+    theirs = [jnp.broadcast_to(centres[c : c + 1, :], shape) for c in range(3)]
+    mine = [jnp.take_along_axis(t, first + rows, axis=1) for t in theirs]
+    d0, d1, d2 = (m - t for m, t in zip(mine, theirs))
+    mirrored = mine[2] + theirs[2]
+    direct_sq = d0 * d0 + d1 * d1 + d2 * d2
+    image_sq = d0 * d0 + d1 * d1 + mirrored * mirrored
+    kernel = 1.0 / jnp.sqrt(direct_sq + 1.0) + 1.0 / jnp.sqrt(image_sq + 1.0)
+    return jnp.where(jnp.abs(first + rows - q) > reach, kernel, 0.0)
+
+
 def sweep_kernel(
     colour_now,
     last,
-    index,
+    near_bubble,
+    near_block,
+    near_count,
     colour,
+    centres,
     before,
     own,
     after,
     moments,
-    far_weight,
     spread_map,
     right_side,
     relaxed,
@@ -73,63 +94,48 @@
     *refs,
 ):
     if last:
-        out, sources, vals, invs, acc, sem_v, sem_i = refs
+        out, sources, acc = refs
     else:
-        out, message, sources, vals, invs, acc, sem_v, sem_i = refs
+        out, message, sources, acc = refs
     bub, nblk, slots, blk, _ = near_vals.shape
     peers = own.shape[0]
     k = blk // bub
-
-    def copy_v(b):
-        return pltpu.make_async_copy(near_vals.at[b], vals.at[b], sem_v.at[b])
-
-    def copy_i(b):
-        return pltpu.make_async_copy(inv_diag.at[b], invs.at[b], sem_i.at[b])
-
-    for b in range(bub):
-
-        @pl.when(colour[b] == colour_now)
-        def _():
-            copy_v(b).start()
-
-    for b in range(bub):
-
-        @pl.when(colour[b] == colour_now)
-        def _():
-            copy_i(b).start()
-
+    none = 3 * peers * nblk * bub
     rows = row_ids((bub, blk))
     for o, ref in enumerate((before, own, after)):
         for p in range(peers):
             for j in range(nblk):
                 at = ((o * peers + p) * nblk + j) * bub
                 sources[at : at + bub, :] = ref[p, j].astype(jnp.float32)
-    sources[3 * peers * nblk * bub :, :] = jnp.zeros((bub, blk), jnp.float32)
+    sources[none:, :] = jnp.zeros((bub, blk), jnp.float32)
     acc[...] = jnp.zeros_like(acc)
 
-    g = far_weight[0] * moments[0]
-    for q in range(1, moments.shape[0]):
-        g = g + far_weight[q] * moments[q]
+    first = lax.axis_index("bubble") * bub
+    weight = far_weights(centres, first, bub)
+    lane = lax.broadcasted_iota(jnp.int32, (bub, blk), 1)
+    g = jnp.zeros((bub, blk), jnp.float32)
+    for q in range(moments.shape[0]):
+        g = g + jnp.take_along_axis(weight, q * bub + lane // k, axis=1) * moments[q]
     shift = blk // 2
     while shift >= k:
         g = g + pltpu.roll(g, shift, 1)
         shift //= 2
-    mine = lax.broadcasted_iota(jnp.int32, (bub, blk), 1) // k == rows
-    coeff = jnp.where(mine, g, 0.0).astype(jnp.bfloat16)
+    coeff = jnp.where(lane // k == rows, g, 0.0).astype(jnp.bfloat16)
     far = lax.dot_general(coeff, spread_map[...], NN, preferred_element_type=jnp.float32)
 
     def near_of(b, carry):
         @pl.when(colour[b] == colour_now)
         def _():
-            copy_v(b).wait()
             here = rows == b
             for r in range(nblk):
                 total = acc[r]
                 for s in range(slots):
-                    i = index[(b * nblk + r) * slots + s]
+                    local = near_bubble[r, s, b] - (first - bub)
+                    row = ((local >> shift_of(bub)) * peers * nblk + near_block[r, s, b]) * bub
+                    i = jnp.where(s < near_count[b, r], row + (local & (bub - 1)), none)
                     src = jnp.where(here, sources[pl.ds(i, 1), :], 0.0).astype(jnp.bfloat16)
                     total = total + lax.dot_general(
-                        src, vals[b, r, s], NT, preferred_element_type=jnp.float32
+                        src, near_vals[b, r, s], NT, preferred_element_type=jnp.float32
                     )
                 acc[r] = total
 
@@ -144,13 +150,12 @@
     def solve(b, carry):
         @pl.when(colour[b] == colour_now)
         def _():
-            copy_i(b).wait()
             here = rows == b
             for r in range(nblk):
                 cols = slice(r * blk, (r + 1) * blk)
                 rest = jnp.where(here, acc[r], 0.0).astype(jnp.bfloat16)
                 out[:, cols] += lax.dot_general(
-                    rest, invs[b, r], NT, preferred_element_type=jnp.float32
+                    rest, inv_diag[b, r], NT, preferred_element_type=jnp.float32
                 )
 
         return carry
@@ -170,25 +175,12 @@
         emit_message(tiles, moment_map, message)
 
 
-def far_weights(centres, my_bubbles, reach, k):
-    n_bub, total = my_bubbles.shape[0], centres.shape[1]
-    groups = total // n_bub
-    theirs = jnp.repeat(centres, k, axis=1).reshape(3, groups, 1, n_bub * k)
-    mine = centres[:, my_bubbles].reshape(3, 1, n_bub, 1)
-    diff = mine - theirs
-    direct_sq = diff[0] * diff[0] + diff[1] * diff[1] + diff[2] * diff[2]
-    mirrored = mine[2] + theirs[2]
-    image_sq = diff[0] * diff[0] + diff[1] * diff[1] + mirrored * mirrored
-    kernel = 1.0 / jnp.sqrt(direct_sq + 1.0) + 1.0 / jnp.sqrt(image_sq + 1.0)
-    lane = lax.broadcasted_iota(jnp.int32, kernel.shape, 2)
-    q = lax.broadcasted_iota(jnp.int32, kernel.shape, 0) * n_bub + lane // k
-    gap = jnp.abs(my_bubbles.reshape(1, n_bub, 1) - q)
-    return jnp.where(gap > reach, kernel, jnp.zeros_like(kernel))
-
-
 VMEM = pl.BlockSpec(memory_space=pltpu.VMEM)
 SMEM = pl.BlockSpec(memory_space=pltpu.SMEM)
-ANY = pl.BlockSpec(memory_space=pl.ANY)
+
+
+def limit(mib):
+    return pltpu.CompilerParams(vmem_limit_bytes=mib << 20)
 
 
 def per_device(
@@ -208,16 +200,8 @@
     k = moment_map.shape[1]
     panels = nblk * blk
     peers, groups = lax.axis_size("panel"), lax.axis_size("bubble")
-    my_index = lax.axis_index("bubble")
-    my_bubbles = my_index * bub + jnp.arange(bub, dtype=jnp.int32)
-    far_weight = far_weights(centres, my_bubbles, bub, k)
     moment_map = moment_map.reshape(bub * k, panels)
     spread_map = spread_map.reshape(bub * k, panels)
-
-    local = near_bubble - (my_index * bub - bub)
-    row = ((local // bub) * peers * nblk + near_block) * bub + local % bub
-    live = jnp.arange(slots)[None, None, :] < near_count[:, :, None]
-    index = jnp.where(live, row, 3 * peers * nblk * bub).reshape(-1)
 
     message_shape = jax.ShapeDtypeStruct((peers, nblk + 1, bub, blk), jnp.bfloat16)
     relaxed_shape = jax.ShapeDtypeStruct((bub, panels), jnp.float32)
@@ -225,8 +209,16 @@
     down = [(j, i) for i, j in up]
 
     message = pl.pallas_call(
-        first_kernel, out_shape=message_shape, in_specs=[VMEM, VMEM], out_specs=VMEM, name="first"
+        first_kernel,
+        out_shape=message_shape,
+        in_specs=[VMEM, VMEM],
+        out_specs=VMEM,
+        compiler_params=limit(2),
+        cost_estimate=pl.CostEstimate(flops=1 << 34, bytes_accessed=1 << 20, transcendentals=0),
+        name="first",
     )(density, moment_map)
+    near_bubble = near_bubble.transpose(1, 2, 0)
+    near_block = near_block.transpose(1, 2, 0)
     relaxed = density
     for colour_now in range(2):
         last = colour_now == 1
@@ -238,31 +230,31 @@
             out_shape=jax.ShapeDtypeStruct((groups, 1, blk), jnp.float32),
             in_specs=[VMEM],
             out_specs=VMEM,
+            compiler_params=limit(2),
             name="moments",
         )(received)
         moments = lax.all_to_all(own_moments, "bubble", 0, 0, tiled=True)
         outs = pl.pallas_call(
             functools.partial(sweep_kernel, colour_now, last),
             out_shape=[relaxed_shape] if last else [relaxed_shape, message_shape],
-            in_specs=[SMEM, SMEM] + [VMEM] * 9 + [ANY, ANY],
+            in_specs=[SMEM] * 4 + [VMEM] * 11,
             out_specs=[VMEM] if last else [VMEM, VMEM],
             scratch_shapes=[
                 pltpu.VMEM(((3 * peers * nblk + 1) * bub, blk), jnp.float32),
-                pltpu.VMEM((bub, nblk, slots, blk, blk), jnp.bfloat16),
-                pltpu.VMEM((bub, nblk, blk, blk), jnp.bfloat16),
                 pltpu.VMEM((nblk, bub, blk), jnp.float32),
-                pltpu.SemaphoreType.DMA((bub,)),
-                pltpu.SemaphoreType.DMA((bub,)),
             ],
+            compiler_params=limit(4),
             name=f"sweep{colour_now}",
         )(
-            index,
+            near_bubble,
+            near_block,
+            near_count,
             colour,
+            centres,
             before,
             received,
             after,
             moments,
-            far_weight,
             spread_map,
             right_side,
             relaxed,

time: 88.9 us -> 78.5 us (0.88)
  the two profiles are of different devices: /device:TPU:8 before, /device:TPU:32 now
where the time goes in v2:
time: 78.5 us; the launch traced here: 77.1 us
  blocking collectives  60.1 us (77%)
  Pallas kernels  10.2 us (13%)
  starting transfers between devices  4.95 us (6%)
  local copies, waits for them, and re-layouts  1.71 us (2%)
    all_to_all x2, blocking collectives, per_device(): moments = lax.all_to_all(own_moments, 'bubble', 0, 0, tiled=True)  37 us
    all_to_all x2, blocking collectives, per_device(): received = lax.all_to_all(message, 'panel', 0, 0, tiled=True)  23.1 us
    pallas_call x2, Pallas kernels, per_device(): pl.pallas_call(functools.partial(sweep_kernel, colour_now, last), out_sha...  9.93 us
    ppermute x2, starting transfers between devices, per_device(): after = lax.ppermute(received, 'bubble', down)  3.03 us
    ppermute x2, starting transfers between devices, per_device(): before = lax.ppermute(received, 'bubble', up)  1.92 us
    unnamed x26, local copies, waits for them, and re-layouts  1.71 us
  transfers between devices with their start and end apart: 4, of which 0 were waited for; matrix products, arithmetic and copies ran while one was open for 0% of the time, Pallas kernels for 0%

profile of v2, /device:TPU:32, one launch (start us, length us, event | category | flops | bytes accessed | tf_op | source)
XLA Modules:
  0.0 77.1 jit_solution(17906278841443989795)
XLA Ops:
  0.0 0.9 %copy-done.2 = bf16[8,16,768]{2,1,0:T(8,128)(2,1)S(1)} copy-done((bf16[8,16,768]{2,1,0:T(8,128)(2,1)S(1)}, bf16[8,16,768]{2,1,0:T(8,128)(2,1)}, u32[]{:S(2)}) %copy-start.2) | copy-done | bytes 196632
  0.9 0.7 copy-done.8
  1.7 0.0 copy-start.5
  1.7 0.0 copy-start.6
  1.7 0.0 copy-start.7
  1.7 0.0 copy-start.9
  1.7 0.0 copy-start.10
  1.7 0.0 copy-start.11
  1.7 0.0 copy-start.12
  1.7 0.2 first.1
  2.0 13.0 %all_to_all.20.received.own = bf16[16,7,8,128]{3,2,1,0:T(8,128)(2,1)S(1)} all-to-all(bf16[16,7,8,128]{3,2,1,0:T(8,128)(2,1)S(1)} %first.1), channel_id=1, replica_groups=mesh['bubble'=16,'panel'=16] {'panel'}, dimensions={0} | all-to-all | bytes 458752 | tf_op jit(solution)/shard_map/all_to_all | solution.py:225
  14.9 0.1 collective-permute-start.1
  15.1 1.9 %collective-permute-start = (bf16[16,7,8,128]{3,2,1,0:T(8,128)(2,1)S(1)}, bf16[16,7,8,128]{3,2,1,0:T(8,128)(2,1)S(1)}, u32[]{:S(2)}, u32[]{:S(2)}) collective-permute-start(bf16[16,7,8,128]{3,2,1,0:T(8,128)(2,1)S(1)} %all_to_all.20.received.own), channel_id=1, source_target_pairs={{0,16},{16,32},{32,48},{48,64},{64,80},{80,96},{96,112},{112,128},... | collective-permute-start | bytes 688136 | tf_op jit(solution)/shard_map/ppermute | solution.py:226
  17.0 21.6 %all_to_all.21.moments = f32[16,1,128]{2,1,0:T(1,128)S(1)} all-to-all(f32[16,1,128]{2,1,0:T(1,128)S(1)} %moments.2), channel_id=1, replica_groups=mesh['bubble'=16,'panel'=16] {'bubble'}, dimensions={0} | all-to-all | bytes 16384 | tf_op jit(solution)/shard_map/all_to_all | solution.py:236
  38.7 0.0 collective-permute-done.1.after
  38.7 0.0 collective-permute-done.before
  38.8 4.0 %sweep0.1 = (f32[8,768]{1,0:T(8,128)S(1)}, bf16[16,7,8,128]{3,2,1,0:T(8,128)(2,1)S(1)}) custom-call(s32[6,4,8]{2,1,0:T(4,128)S(1)} %bitcast.9, s32[6,4,8]{2,1,0:T(4,128)S(1)} %bitcast.11, s32[8,6]{1,0:T(8,128)S(1)} %copy-done.10, s32[8]{0:T(128)S(1)} %copy-done.12, f32[3,128]{1,0:T(4,128)S(1)} %copy-done.11, ...), custom_call_target="tpu_custom_call" | custom-call | tf_op jit(solution)/shard_map/sweep0/pallas_call | solution.py:237
  42.8 10.1 %all_to_all.22.received.own = bf16[16,7,8,128]{3,2,1,0:T(8,128)(2,1)S(1)} all-to-all(bf16[16,7,8,128]{3,2,1,0:T(8,128)(2,1)S(1)} %get-tuple-element.7), channel_id=1, replica_groups=mesh['bubble'=16,'panel'=16] {'panel'}, dimensions={0} | all-to-all | bytes 458752 | tf_op jit(solution)/shard_map/all_to_all | solution.py:225
  52.9 2.9 %collective-permute-start.3 = (bf16[16,7,8,128]{3,2,1,0:T(8,128)(2,1)S(1)}, bf16[16,7,8,128]{3,2,1,0:T(8,128)(2,1)S(1)}, u32[]{:S(2)}, u32[]{:S(2)}) collective-permute-start(bf16[16,7,8,128]{3,2,1,0:T(8,128)(2,1)S(1)} %all_to_all.22.received.own), channel_id=1, source_target_pairs={{16,0},{32,16},{48,32},{64,48},{80,64},{96,80},{112,96},{128,112},... | collective-permute-start | bytes 688136 | tf_op jit(solution)/shard_map/ppermute | solution.py:227
  55.8 0.0 collective-permute-start.2
  55.8 15.4 %all_to_all.23.moments = f32[16,1,128]{2,1,0:T(1,128)S(1)} all-to-all(f32[16,1,128]{2,1,0:T(1,128)S(1)} %moments.3), channel_id=1, replica_groups=mesh['bubble'=16,'panel'=16] {'bubble'}, dimensions={0} | all-to-all | bytes 16384 | tf_op jit(solution)/shard_map/all_to_all | solution.py:236
  71.2 0.0 collective-permute-done.3.after
  71.2 0.0 collective-permute-done.2.before
  71.2 5.9 %sweep1.1 = f32[8,768]{1,0:T(8,128)} custom-call(s32[6,4,8]{2,1,0:T(4,128)S(1)} %bitcast.10, s32[6,4,8]{2,1,0:T(4,128)S(1)} %bitcast.12, s32[8,6]{1,0:T(8,128)S(1)} %copy-done.10, s32[8]{0:T(128)S(1)} %copy-done.12, f32[3,128]{1,0:T(4,128)S(1)} %copy-done.11, bf16[16,7,8,128]{3,2,1,0:T(8,128)(2,1)S(1)} %collective-permute-done.2.before, ...), custom_call_target="tpu_custom_call" | custom-call | tf_op jit(solution)/shard_map/sweep1/pallas_call | solution.py:237
  (19 shorter events, 0.1 us)
Async XLA Ops:
  0.0 0.9 %copy-start.2 = (bf16[8,16,768]{2,1,0:T(8,128)(2,1)S(1)}, bf16[8,16,768]{2,1,0:T(8,128)(2,1)}, u32[]{:S(2)}) copy-start(bf16[8,16,768]{2,1,0:T(8,128)(2,1)} %param.19) | copy-start | bytes 589828
  0.9 0.7 copy-start.8
  1.7 37.0 %copy-start = (bf16[8,6,4,128,128]{4,3,2,1,0:T(8,128)(2,1)S(1)}, bf16[8,6,4,128,128]{4,3,2,1,0:T(8,128)(2,1)}, u32[]{:S(2)}) copy-start(bf16[8,6,4,128,128]{4,3,2,1,0:T(8,128)(2,1)} %near_vals.3) | copy-start | bytes 18874372
  1.7 37.0 %copy-start.1 = (bf16[8,6,128,128]{3,2,1,0:T(8,128)(2,1)S(1)}, bf16[8,6,128,128]{3,2,1,0:T(8,128)(2,1)}, u32[]{:S(2)}) copy-start(bf16[8,6,128,128]{3,2,1,0:T(8,128)(2,1)} %inv_diag.3) | copy-start | bytes 4718596
  1.7 37.0 %copy-start.3 = (bf16[8,16,768]{2,1,0:T(8,128)(2,1)S(1)}, bf16[8,16,768]{2,1,0:T(8,128)(2,1)}, u32[]{:S(2)}) copy-start(bf16[8,16,768]{2,1,0:T(8,128)(2,1)} %param.19) | copy-start | bytes 589828
  1.7 37.0 %copy-start.4 = (bf16[8,16,768]{2,1,0:T(8,128)(2,1)S(1)}, bf16[8,16,768]{2,1,0:T(8,128)(2,1)}, u32[]{:S(2)}) copy-start(bf16[8,16,768]{2,1,0:T(8,128)(2,1)} %param.20) | copy-start | bytes 589828
  1.7 37.0 %copy-start.5 = (f32[8,768]{1,0:T(8,128)S(1)}, f32[8,768]{1,0:T(8,128)}, u32[]{:S(2)}) copy-start(f32[8,768]{1,0:T(8,128)} %right_side.3) | copy-start | bytes 73732
  1.7 37.0 %copy-start.6 = (s32[8,6,4]{0,2,1:T(4,128)S(1)}, s32[8,6,4]{0,2,1:T(4,128)}, u32[]{:S(2)}) copy-start(s32[8,6,4]{0,2,1:T(4,128)} %param.15) | copy-start | bytes 2308
  1.7 37.0 %copy-start.7 = (s32[8,6,4]{0,2,1:T(4,128)S(1)}, s32[8,6,4]{0,2,1:T(4,128)}, u32[]{:S(2)}) copy-start(s32[8,6,4]{0,2,1:T(4,128)} %param.16) | copy-start | bytes 2308
  1.7 37.0 %copy-start.9 = (f32[8,768]{1,0:T(8,128)S(1)}, f32[8,768]{1,0:T(8,128)}, u32[]{:S(2)}) copy-start(f32[8,768]{1,0:T(8,128)} %relaxed.1) | copy-start | bytes 73732
  1.7 37.0 %copy-start.10 = (s32[8,6]{1,0:T(8,128)S(1)}, s32[8,6]{1,0:T(8,128)}, u32[]{:S(2)}) copy-start(s32[8,6]{1,0:T(8,128)} %near_count.3) | copy-start | bytes 580
  1.7 37.0 %copy-start.11 = (f32[3,128]{1,0:T(4,128)S(1)}, f32[3,128]{1,0:T(4,128)}, u32[]{:S(2)}) copy-start(f32[3,128]{1,0:T(4,128)} %centres.3) | copy-start | bytes 4612
  1.7 37.0 %copy-start.12 = (s32[8]{0:T(128)S(1)}, s32[8]{0:T(128)}, u32[]{:S(2)}) copy-start(s32[8]{0:T(128)} %colour.3) | copy-start | bytes 100
  14.9 23.7 %collective-permute-start.1 = (bf16[16,7,8,128]{3,2,1,0:T(8,128)(2,1)S(1)}, bf16[16,7,8,128]{3,2,1,0:T(8,128)(2,1)S(1)}, u32[]{:S(2)}, u32[]{:S(2)}) collective-permute-start(bf16[16,7,8,128]{3,2,1,0:T(8,128)(2,1)S(1)} %all_to_all.20.received.own), channel_id=1, source_target_pairs={{16,0},{32,16},{48,32},{64,48},{80,64},{96,80},{112,96},{128,112},... | collective-permute-start | bytes 688136 | tf_op jit(solution)/shard_map/ppermute | solution.py:227
  15.1 23.6 %collective-permute-start = (bf16[16,7,8,128]{3,2,1,0:T(8,128)(2,1)S(1)}, bf16[16,7,8,128]{3,2,1,0:T(8,128)(2,1)S(1)}, u32[]{:S(2)}, u32[]{:S(2)}) collective-permute-start(bf16[16,7,8,128]{3,2,1,0:T(8,128)(2,1)S(1)} %all_to_all.20.received.own), channel_id=1, source_target_pairs={{0,16},{16,32},{32,48},{48,64},{64,80},{80,96},{96,112},{112,128},... | collective-permute-start | bytes 688136 | tf_op jit(solution)/shard_map/ppermute | solution.py:226
  52.9 18.3 %collective-permute-start.3 = (bf16[16,7,8,128]{3,2,1,0:T(8,128)(2,1)S(1)}, bf16[16,7,8,128]{3,2,1,0:T(8,128)(2,1)S(1)}, u32[]{:S(2)}, u32[]{:S(2)}) collective-permute-start(bf16[16,7,8,128]{3,2,1,0:T(8,128)(2,1)S(1)} %all_to_all.22.received.own), channel_id=1, source_target_pairs={{16,0},{32,16},{48,32},{64,48},{80,64},{96,80},{112,96},{128,112},... | collective-permute-start | bytes 688136 | tf_op jit(solution)/shard_map/ppermute | solution.py:227
  55.8 15.4 %collective-permute-start.2 = (bf16[16,7,8,128]{3,2,1,0:T(8,128)(2,1)S(1)}, bf16[16,7,8,128]{3,2,1,0:T(8,128)(2,1)S(1)}, u32[]{:S(2)}, u32[]{:S(2)}) collective-permute-start(bf16[16,7,8,128]{3,2,1,0:T(8,128)(2,1)S(1)} %all_to_all.22.received.own), channel_id=1, source_target_pairs={{0,16},{16,32},{32,48},{48,64},{64,80},{80,96},{96,112},{112,128},... | collective-permute-start | bytes 688136 | tf_op jit(solution)/shard_map/ppermute | solution.py:226

commit v3 on v2

--- a/solution.py
+++ b/solution.py
@@ -6,6 +6,7 @@
 from jax.experimental import pallas as pl
 from jax.experimental.pallas import tpu as pltpu
 from jax.sharding import PartitionSpec as P
+
 
 NT = (((1,), (1,)), ((), ()))
 NN = (((1,), (0,)), ((), ()))
@@ -37,7 +38,15 @@
             message[p, j] = blocks[j]
 
 
-def first_kernel(density, moment_map, message):
+def first_kernel(density_hbm, map_hbm, message, density, moment_map, sems):
+    copies = [
+        pltpu.make_async_copy(map_hbm, moment_map, sems.at[0]),
+        pltpu.make_async_copy(density_hbm, density, sems.at[1]),
+    ]
+    for c in copies:
+        c.start()
+    for c in copies:
+        c.wait()
     n = message.shape[1] - 1
     w = message.shape[3]
     tiles = [density[:, j * w : (j + 1) * w] for j in range(n)]
@@ -73,42 +82,87 @@
     return jnp.where(jnp.abs(first + rows - q) > reach, kernel, 0.0)
 
 
-def sweep_kernel(
+def near_kernel(
     colour_now,
-    last,
     near_bubble,
     near_block,
     near_count,
     colour,
-    centres,
-    before,
+    odd_swap,
     own,
-    after,
-    moments,
-    spread_map,
-    right_side,
-    relaxed,
-    moment_map,
+    even_swap,
     near_vals,
-    inv_diag,
-    *refs,
+    acc,
+    sources,
+    vals,
+    sems,
 ):
-    if last:
-        out, sources, acc = refs
-    else:
-        out, message, sources, acc = refs
     bub, nblk, slots, blk, _ = near_vals.shape
     peers = own.shape[0]
-    k = blk // bub
+    my_index = lax.axis_index("bubble")
+    first = my_index * bub
+    even = (my_index & 1) == 0
     none = 3 * peers * nblk * bub
+
+    def copy(b):
+        return pltpu.make_async_copy(near_vals.at[b], vals.at[b], sems.at[b])
+
+    for b in range(bub):
+
+        @pl.when(colour[b] == colour_now)
+        def _():
+            copy(b).start()
+
     rows = row_ids((bub, blk))
-    for o, ref in enumerate((before, own, after)):
+    for o, ref in enumerate((odd_swap, own, even_swap)):
         for p in range(peers):
             for j in range(nblk):
                 at = ((o * peers + p) * nblk + j) * bub
                 sources[at : at + bub, :] = ref[p, j].astype(jnp.float32)
     sources[none:, :] = jnp.zeros((bub, blk), jnp.float32)
     acc[...] = jnp.zeros_like(acc)
+
+    def near_of(b, carry):
+        @pl.when(colour[b] == colour_now)
+        def _():
+            copy(b).wait()
+            here = rows == b
+            for r in range(nblk):
+                picked = []
+                for s in range(slots):
+                    local = near_bubble[r, s, b] - (first - bub)
+                    o = local >> shift_of(bub)
+                    o = jnp.where(even, o, 2 - o)
+                    row = (o * peers * nblk + near_block[r, s, b]) * bub + (local & (bub - 1))
+                    i = jnp.where(s < near_count[b, r], row, none)
+                    picked.append(jnp.where(here, sources[pl.ds(i, 1), :], 0.0))
+                src = jnp.concatenate(picked, axis=1).astype(jnp.bfloat16)
+                block = jnp.concatenate([vals[b, r, s] for s in range(slots)], axis=1)
+                acc[r] += lax.dot_general(src, block, NT, preferred_element_type=jnp.float32)
+
+        return carry
+
+    lax.fori_loop(0, bub, near_of, 0)
+
+
+def finish_kernel(
+    colour_now,
+    last,
+    colour,
+    centres,
+    moments,
+    near,
+    spread_map,
+    right_side,
+    relaxed,
+    moment_map,
+    inv_diag,
+    *refs,
+):
+    bub, nblk, blk, _ = inv_diag.shape
+    k = blk // bub
+    out = refs[0]
+    rows = row_ids((bub, blk))
 
     first = lax.axis_index("bubble") * bub
     weight = far_weights(centres, first, bub)
@@ -123,44 +177,6 @@
     coeff = jnp.where(lane // k == rows, g, 0.0).astype(jnp.bfloat16)
     far = lax.dot_general(coeff, spread_map[...], NN, preferred_element_type=jnp.float32)
 
-    def near_of(b, carry):
-        @pl.when(colour[b] == colour_now)
-        def _():
-            here = rows == b
-            for r in range(nblk):
-                total = acc[r]
-                for s in range(slots):
-                    local = near_bubble[r, s, b] - (first - bub)
-                    row = ((local >> shift_of(bub)) * peers * nblk + near_block[r, s, b]) * bub
-                    i = jnp.where(s < near_count[b, r], row + (local & (bub - 1)), none)
-                    src = jnp.where(here, sources[pl.ds(i, 1), :], 0.0).astype(jnp.bfloat16)
-                    total = total + lax.dot_general(
-                        src, near_vals[b, r, s], NT, preferred_element_type=jnp.float32
-                    )
-                acc[r] = total
-
-        return carry
-
-    lax.fori_loop(0, bub, near_of, 0)
-    for r in range(nblk):
-        cols = slice(r * blk, (r + 1) * blk)
-        acc[r] = right_side[:, cols] - acc[r] - far[:, cols]
-        out[:, cols] = jnp.zeros((bub, blk), jnp.float32)
-
-    def solve(b, carry):
-        @pl.when(colour[b] == colour_now)
-        def _():
-            here = rows == b
-            for r in range(nblk):
-                cols = slice(r * blk, (r + 1) * blk)
-                rest = jnp.where(here, acc[r], 0.0).astype(jnp.bfloat16)
-                out[:, cols] += lax.dot_general(
-                    rest, inv_diag[b, r], NT, preferred_element_type=jnp.float32
-                )
-
-        return carry
-
-    lax.fori_loop(0, bub, solve, 0)
     colours = jnp.zeros((bub, blk), jnp.int32)
     for b in range(bub):
         colours = jnp.where(rows == b, colour[b], colours)
@@ -168,15 +184,31 @@
     tiles = []
     for r in range(nblk):
         cols = slice(r * blk, (r + 1) * blk)
-        tile = jnp.where(live, out[:, cols], relaxed[:, cols])
+        rest = right_side[:, cols] - near[r] - far[:, cols]
+        rest = jnp.where(live, rest, 0.0)
+        updated = jnp.zeros((bub, blk), jnp.float32)
+        for b in range(0, bub, 2):
+            pair = jnp.concatenate(
+                [jnp.where(rows == b, rest, 0.0), jnp.where(rows == b + 1, rest, 0.0)], axis=1
+            ).astype(jnp.bfloat16)
+            block = jnp.concatenate([inv_diag[b, r], inv_diag[b + 1, r]], axis=1)
+            updated = updated + lax.dot_general(
+                pair, block, NT, preferred_element_type=jnp.float32
+            )
+        tile = jnp.where(live, updated, relaxed[:, cols])
         out[:, cols] = tile
         tiles.append(tile)
     if not last:
-        emit_message(tiles, moment_map, message)
+        emit_message(tiles, moment_map, refs[1])
 
 
 VMEM = pl.BlockSpec(memory_space=pltpu.VMEM)
 SMEM = pl.BlockSpec(memory_space=pltpu.SMEM)
+HBM = pl.BlockSpec(memory_space=pltpu.HBM)
+
+
+def in_hbm(x):
+    return pltpu.with_memory_space_constraint(x, pltpu.HBM)
 
 
 def limit(mib):
@@ -205,26 +237,33 @@
 
     message_shape = jax.ShapeDtypeStruct((peers, nblk + 1, bub, blk), jnp.bfloat16)
     relaxed_shape = jax.ShapeDtypeStruct((bub, panels), jnp.float32)
-    up = [(i, (i + 1) % groups) for i in range(groups)]
-    down = [(j, i) for i, j in up]
+    pairs = [(i, i + 1) for i in range(groups - 1)]
+    odd_pairs = [(i, j) for p in pairs[1::2] for i, j in (p, p[::-1])]
+    even_pairs = [(i, j) for p in pairs[0::2] for i, j in (p, p[::-1])]
 
     message = pl.pallas_call(
         first_kernel,
         out_shape=message_shape,
-        in_specs=[VMEM, VMEM],
+        in_specs=[HBM, HBM],
         out_specs=VMEM,
+        scratch_shapes=[
+            pltpu.VMEM((bub, panels), jnp.float32),
+            pltpu.VMEM((bub * k, panels), jnp.bfloat16),
+            pltpu.SemaphoreType.DMA((2,)),
+        ],
         compiler_params=limit(2),
         cost_estimate=pl.CostEstimate(flops=1 << 34, bytes_accessed=1 << 20, transcendentals=0),
         name="first",
-    )(density, moment_map)
+    )(in_hbm(density), in_hbm(moment_map))
+    near_vals = in_hbm(near_vals)
     near_bubble = near_bubble.transpose(1, 2, 0)
     near_block = near_block.transpose(1, 2, 0)
     relaxed = density
     for colour_now in range(2):
         last = colour_now == 1
         received = lax.all_to_all(message, "panel", 0, 0, tiled=True)
-        before = lax.ppermute(received, "bubble", up)
-        after = lax.ppermute(received, "bubble", down)
+        odd_swap = lax.ppermute(received, "bubble", odd_pairs)
+        even_swap = lax.ppermute(received, "bubble", even_pairs)
         own_moments = pl.pallas_call(
             moment_kernel,
             out_shape=jax.ShapeDtypeStruct((groups, 1, blk), jnp.float32),
@@ -234,34 +273,25 @@
             name="moments",
         )(received)
         moments = lax.all_to_all(own_moments, "bubble", 0, 0, tiled=True)
-        outs = pl.pallas_call(
-            functools.partial(sweep_kernel, colour_now, last),
-            out_shape=[relaxed_shape] if last else [relaxed_shape, message_shape],
-            in_specs=[SMEM] * 4 + [VMEM] * 11,
-            out_specs=[VMEM] if last else [VMEM, VMEM],
+        near = pl.pallas_call(
+            functools.partial(near_kernel, colour_now),
+            out_shape=jax.ShapeDtypeStruct((nblk, bub, blk), jnp.float32),
+            in_specs=[SMEM] * 4 + [VMEM] * 3 + [HBM],
+            out_specs=VMEM,
             scratch_shapes=[
                 pltpu.VMEM(((3 * peers * nblk + 1) * bub, blk), jnp.float32),
-                pltpu.VMEM((nblk, bub, blk), jnp.float32),
+                pltpu.VMEM((bub, nblk, slots, blk, blk), jnp.bfloat16),
+                pltpu.SemaphoreType.DMA((bub,)),
             ],
+            compiler_params=limit(12),
+        )(near_bubble, near_block, near_count, colour, odd_swap, received, even_swap, near_vals)
+        outs = pl.pallas_call(
+            functools.partial(finish_kernel, colour_now, last),
+            out_shape=[relaxed_shape] if last else [relaxed_shape, message_shape],
+            in_specs=[SMEM] + [VMEM] * 8,
+            out_specs=[VMEM] if last else [VMEM, VMEM],
             compiler_params=limit(4),
-            name=f"sweep{colour_now}",
-        )(
-            near_bubble,
-            near_block,
-            near_count,
-            colour,
-            centres,
-            before,
-            received,
-            after,
-            moments,
-            spread_map,
-            right_side,
-            relaxed,
-            moment_map,
-            near_vals,
-            inv_diag,
-        )
+        )(colour, centres, moments, near, spread_map, right_side, relaxed, moment_map, inv_diag)
         if last:
             (relaxed,) = outs
         else:
@@ -284,6 +314,7 @@
         P(),
     )
     out_specs = P("bubble", "panel")
+
     return jax.shard_map(
         per_device, mesh=mesh, in_specs=in_specs, out_specs=out_specs, check_vma=False
     )

time: 78.5 us -> 71.9 us (0.916)
  the two profiles are of different devices: /device:TPU:32 before, /device:TPU:8 now
where the time goes in v3:
time: 71.9 us; the launch traced here: 71.6 us
  starting transfers between devices  22.7 us (32%)
  blocking collectives  22.5 us (31%)
  Pallas kernels  13.4 us (19%)
  waiting for transfers between devices  12.7 us (18%)
    all_to_all x2, blocking collectives, per_device(): received = lax.all_to_all(message, 'panel', 0, 0, tiled=True)  22.5 us
    all_to_all x2, starting transfers between devices, per_device(): moments = lax.all_to_all(own_moments, 'bubble', 0, 0, tiled=True)  13.8 us
    all_to_all x2, waiting for transfers between devices, per_device(): moments = lax.all_to_all(own_moments, 'bubble', 0, 0, tiled=True)  12.7 us
    ppermute x2, starting transfers between devices, per_device(): even_swap = lax.ppermute(received, 'bubble', even_pairs)  7.66 us
    pallas_call x2, Pallas kernels, per_device(): pl.pallas_call(functools.partial(near_kernel, colour_now), out_shape=jax....  7.04 us
    pallas_call x2, Pallas kernels, per_device(): pl.pallas_call(functools.partial(finish_kernel, colour_now, last), out_sh...  3.91 us
  transfers between devices with their start and end apart: 6, of which 2 were waited for; matrix products, arithmetic and copies ran while one was open for 0% of the time, Pallas kernels for 12%

profile of v3, /device:TPU:8, one launch (start us, length us, event | category | flops | bytes accessed | tf_op | source)
XLA Modules:
  0.0 71.6 jit_solution(17608433026092750553)
XLA Ops:
  0.0 1.2 %first.1 = bf16[16,7,8,128]{3,2,1,0:T(8,128)(2,1)S(1)} custom-call(f32[8,768]{1,0:T(8,128)} %relaxed.1, bf16[128,768]{1,0:T(8,128)(2,1)} %bitcast.4), custom_call_target="tpu_custom_call" | custom-call | flops 17179869184 | bytes 1048576 | tf_op jit(solution)/shard_map/first/pallas_call | solution.py:244
  1.2 0.0 copy-start
  1.2 0.0 copy-start.1
  1.2 0.0 copy-start.2
  1.3 0.0 copy-start.3
  1.3 0.0 copy-start.6
  1.3 0.0 copy-start.8
  1.3 11.8 %all_to_all.20.received.own = bf16[16,7,8,128]{3,2,1,0:T(8,128)(2,1)S(1)} all-to-all(bf16[16,7,8,128]{3,2,1,0:T(8,128)(2,1)S(1)} %first.1), channel_id=1, replica_groups=mesh['bubble'=16,'panel'=16] {'panel'}, dimensions={0} | all-to-all | bytes 458752 | tf_op jit(solution)/shard_map/all_to_all | solution.py:264
  13.1 0.7 collective-permute-start
  13.8 5.2 %collective-permute-start.1 = (bf16[16,7,8,128]{3,2,1,0:T(8,128)(2,1)S(1)}, bf16[16,7,8,128]{3,2,1,0:T(8,128)(2,1)S(1)}, u32[]{:S(2)}, u32[]{:S(2)}) collective-permute-start(bf16[16,7,8,128]{3,2,1,0:T(8,128)(2,1)S(1)} %all_to_all.20.received.own), channel_id=1, source_target_pairs={{0,16},{16,0},{32,48},{48,32},{64,80},{80,64},{96,112},{112,96},{1... | collective-permute-start | bytes 688136 | tf_op jit(solution)/shard_map/ppermute | solution.py:266
  19.0 0.6 moments.2
  19.6 8.5 %all-to-all-start.1 = ((f32[16,1,128]{2,1,0:T(1,128)}), f32[16,1,128]{2,1,0:T(1,128)S(1)}, u32[]{:S(2)}, u32[]{:S(2)}) async-start(f32[16,1,128]{2,1,0:T(1,128)} %moments.2), calls=%async_computation.1 | async-start | bytes 16384 | tf_op jit(solution)/shard_map/all_to_all | solution.py:275
  28.1 0.0 collective-permute-done.odd_swap
  28.2 3.5 %shard_map.109.near = f32[6,8,128]{2,1,0:T(8,128)S(1)} custom-call(s32[6,4,8]{2,1,0:T(4,128)S(1)} %bitcast.9, s32[6,4,8]{2,1,0:T(4,128)S(1)} %bitcast.11, s32[8,6]{1,0:T(8,128)S(1)} %copy-done.7, s32[8]{0:T(128)S(1)} %copy-done.9, bf16[16,7,8,128]{3,2,1,0:T(8,128)(2,1)S(1)} %collective-permute-done.odd_swap, ...), custom_call_target="tpu_custom_call" | custom-call | tf_op jit(solution)/shard_map/pallas_call | solution.py:276
  31.7 6.3 %all-to-all-done.1.moments = f32[16,1,128]{2,1,0:T(1,128)S(1)} async-done(((f32[16,1,128]{2,1,0:T(1,128)}), f32[16,1,128]{2,1,0:T(1,128)S(1)}, u32[]{:S(2)}, u32[]{:S(2)}) %all-to-all-start.1) | async-done | bytes 8224 | tf_op jit(solution)/shard_map/all_to_all | solution.py:275
  38.1 1.7 %shard_map.110 = (f32[8,768]{1,0:T(8,128)S(1)}, bf16[16,7,8,128]{3,2,1,0:T(8,128)(2,1)S(1)}) custom-call(s32[8]{0:T(128)S(1)} %copy-done.9, f32[3,128]{1,0:T(4,128)S(1)} %copy-done.8, f32[16,1,128]{2,1,0:T(1,128)S(1)} %all-to-all-done.1.moments, f32[6,8,128]{2,1,0:T(8,128)S(1)} %shard_map.109.near, bf16[128,768]{1,0:T(8,128)(2,1)S(1)} %bitcast.7, ...), custom_call_target="tpu_custom_call" | custom-call | tf_op jit(solution)/shard_map/pallas_call | solution.py:288
  39.8 10.7 %all_to_all.21.received.own = bf16[16,7,8,128]{3,2,1,0:T(8,128)(2,1)S(1)} all-to-all(bf16[16,7,8,128]{3,2,1,0:T(8,128)(2,1)S(1)} %get-tuple-element.7), channel_id=1, replica_groups=mesh['bubble'=16,'panel'=16] {'panel'}, dimensions={0} | all-to-all | bytes 458752 | tf_op jit(solution)/shard_map/all_to_all | solution.py:264
  50.5 0.7 collective-permute-start.2
  51.1 2.5 %collective-permute-start.3 = (bf16[16,7,8,128]{3,2,1,0:T(8,128)(2,1)S(1)}, bf16[16,7,8,128]{3,2,1,0:T(8,128)(2,1)S(1)}, u32[]{:S(2)}, u32[]{:S(2)}) collective-permute-start(bf16[16,7,8,128]{3,2,1,0:T(8,128)(2,1)S(1)} %all_to_all.21.received.own), channel_id=1, source_target_pairs={{0,16},{16,0},{32,48},{48,32},{64,80},{80,64},{96,112},{112,96},{1... | collective-permute-start | bytes 688136 | tf_op jit(solution)/shard_map/ppermute | solution.py:266
  53.6 0.6 moments.3
  54.3 5.3 %all-to-all-start.3 = ((f32[16,1,128]{2,1,0:T(1,128)}), f32[16,1,128]{2,1,0:T(1,128)S(1)}, u32[]{:S(2)}, u32[]{:S(2)}) async-start(f32[16,1,128]{2,1,0:T(1,128)} %moments.3), calls=%async_computation.3 | async-start | bytes 16384 | tf_op jit(solution)/shard_map/all_to_all | solution.py:275
  59.5 3.5 %shard_map.111.near = f32[6,8,128]{2,1,0:T(8,128)S(1)} custom-call(s32[6,4,8]{2,1,0:T(4,128)S(1)} %bitcast.10, s32[6,4,8]{2,1,0:T(4,128)S(1)} %bitcast.12, s32[8,6]{1,0:T(8,128)S(1)} %copy-done.7, s32[8]{0:T(128)S(1)} %copy-done.9, bf16[16,7,8,128]{3,2,1,0:T(8,128)(2,1)S(1)} %collective-permute-done.2.odd_swap, ...), custom_call_target="tpu_custom_call" | custom-call | tf_op jit(solution)/shard_map/pallas_call | solution.py:276
  63.1 6.4 %all-to-all-done.3.moments = f32[16,1,128]{2,1,0:T(1,128)S(1)} async-done(((f32[16,1,128]{2,1,0:T(1,128)}), f32[16,1,128]{2,1,0:T(1,128)S(1)}, u32[]{:S(2)}, u32[]{:S(2)}) %all-to-all-start.3) | async-done | bytes 8224 | tf_op jit(solution)/shard_map/all_to_all | solution.py:275
  69.4 2.2 %shard_map.112 = f32[8,768]{1,0:T(8,128)} custom-call(s32[8]{0:T(128)S(1)} %copy-done.9, f32[3,128]{1,0:T(4,128)S(1)} %copy-done.8, f32[16,1,128]{2,1,0:T(1,128)S(1)} %all-to-all-done.3.moments, f32[6,8,128]{2,1,0:T(8,128)S(1)} %shard_map.111.near, bf16[128,768]{1,0:T(8,128)(2,1)S(1)} %bitcast.8, f32[8,768]{1,0:T(8,128)S(1)} %copy-done.3, ...), custom_call_target="tpu_custom_call" | custom-call | tf_op jit(solution)/shard_map/pallas_call | solution.py:288
  (17 shorter events, 0.0 us)
Async XLA Ops:
  0.0 28.1 %copy-start.4 = (s32[8,6,4]{0,2,1:T(4,128)S(1)}, s32[8,6,4]{0,2,1:T(4,128)}, u32[]{:S(2)}) copy-start(s32[8,6,4]{0,2,1:T(4,128)} %param.15) | copy-start | bytes 2308
  0.0 28.1 %copy-start.5 = (s32[8,6,4]{0,2,1:T(4,128)S(1)}, s32[8,6,4]{0,2,1:T(4,128)}, u32[]{:S(2)}) copy-start(s32[8,6,4]{0,2,1:T(4,128)} %param.16) | copy-start | bytes 2308
  0.0 28.1 %copy-start.7 = (s32[8,6]{1,0:T(8,128)S(1)}, s32[8,6]{1,0:T(8,128)}, u32[]{:S(2)}) copy-start(s32[8,6]{1,0:T(8,128)} %near_count.3) | copy-start | bytes 580
  0.0 28.1 %copy-start.9 = (s32[8]{0:T(128)S(1)}, s32[8]{0:T(128)}, u32[]{:S(2)}) copy-start(s32[8]{0:T(128)} %colour.7) | copy-start | bytes 100
  1.2 36.8 %copy-start = (bf16[8,6,128,128]{3,2,1,0:T(8,128)(2,1)S(1)}, bf16[8,6,128,128]{3,2,1,0:T(8,128)(2,1)}, u32[]{:S(2)}) copy-start(bf16[8,6,128,128]{3,2,1,0:T(8,128)(2,1)} %inv_diag.3) | copy-start | bytes 4718596
  1.2 36.8 %copy-start.1 = (bf16[8,16,768]{2,1,0:T(8,128)(2,1)S(1)}, bf16[8,16,768]{2,1,0:T(8,128)(2,1)}, u32[]{:S(2)}) copy-start(bf16[8,16,768]{2,1,0:T(8,128)(2,1)} %param.19) | copy-start | bytes 589828
  1.2 36.8 %copy-start.2 = (bf16[8,16,768]{2,1,0:T(8,128)(2,1)S(1)}, bf16[8,16,768]{2,1,0:T(8,128)(2,1)}, u32[]{:S(2)}) copy-start(bf16[8,16,768]{2,1,0:T(8,128)(2,1)} %param.20) | copy-start | bytes 589828
  1.3 36.8 %copy-start.3 = (f32[8,768]{1,0:T(8,128)S(1)}, f32[8,768]{1,0:T(8,128)}, u32[]{:S(2)}) copy-start(f32[8,768]{1,0:T(8,128)} %right_side.3) | copy-start | bytes 73732
  1.3 36.8 %copy-start.6 = (f32[8,768]{1,0:T(8,128)S(1)}, f32[8,768]{1,0:T(8,128)}, u32[]{:S(2)}) copy-start(f32[8,768]{1,0:T(8,128)} %relaxed.1) | copy-start | bytes 73732
  1.3 36.8 %copy-start.8 = (f32[3,128]{1,0:T(4,128)S(1)}, f32[3,128]{1,0:T(4,128)}, u32[]{:S(2)}) copy-start(f32[3,128]{1,0:T(4,128)} %centres.3) | copy-start | bytes 4612
  13.1 15.0 %collective-permute-start = (bf16[16,7,8,128]{3,2,1,0:T(8,128)(2,1)S(1)}, bf16[16,7,8,128]{3,2,1,0:T(8,128)(2,1)S(1)}, u32[]{:S(2)}, u32[]{:S(2)}) collective-permute-start(bf16[16,7,8,128]{3,2,1,0:T(8,128)(2,1)S(1)} %all_to_all.20.received.own), channel_id=1, source_target_pairs={{16,32},{32,16},{48,64},{64,48},{80,96},{96,80},{112,128},{128,112... | collective-permute-start | bytes 688136 | tf_op jit(solution)/shard_map/ppermute | solution.py:265
  13.8 14.3 %collective-permute-start.1 = (bf16[16,7,8,128]{3,2,1,0:T(8,128)(2,1)S(1)}, bf16[16,7,8,128]{3,2,1,0:T(8,128)(2,1)S(1)}, u32[]{:S(2)}, u32[]{:S(2)}) collective-permute-start(bf16[16,7,8,128]{3,2,1,0:T(8,128)(2,1)S(1)} %all_to_all.20.received.own), channel_id=1, source_target_pairs={{0,16},{16,0},{32,48},{48,32},{64,80},{80,64},{96,112},{112,96},{1... | collective-permute-start | bytes 688136 | tf_op jit(solution)/shard_map/ppermute | solution.py:266
  19.6 18.4 %all-to-all-start.1 = ((f32[16,1,128]{2,1,0:T(1,128)}), f32[16,1,128]{2,1,0:T(1,128)S(1)}, u32[]{:S(2)}, u32[]{:S(2)}) async-start(f32[16,1,128]{2,1,0:T(1,128)} %moments.2), calls=%async_computation.1 | async-start | bytes 16384 | tf_op jit(solution)/shard_map/all_to_all | solution.py:275
  50.5 9.1 %collective-permute-start.2 = (bf16[16,7,8,128]{3,2,1,0:T(8,128)(2,1)S(1)}, bf16[16,7,8,128]{3,2,1,0:T(8,128)(2,1)S(1)}, u32[]{:S(2)}, u32[]{:S(2)}) collective-permute-start(bf16[16,7,8,128]{3,2,1,0:T(8,128)(2,1)S(1)} %all_to_all.21.received.own), channel_id=1, source_target_pairs={{16,32},{32,16},{48,64},{64,48},{80,96},{96,80},{112,128},{128,112... | collective-permute-start | bytes 688136 | tf_op jit(solution)/shard_map/ppermute | solution.py:265
  51.1 8.4 %collective-permute-start.3 = (bf16[16,7,8,128]{3,2,1,0:T(8,128)(2,1)S(1)}, bf16[16,7,8,128]{3,2,1,0:T(8,128)(2,1)S(1)}, u32[]{:S(2)}, u32[]{:S(2)}) collective-permute-start(bf16[16,7,8,128]{3,2,1,0:T(8,128)(2,1)S(1)} %all_to_all.21.received.own), channel_id=1, source_target_pairs={{0,16},{16,0},{32,48},{48,32},{64,80},{80,64},{96,112},{112,96},{1... | collective-permute-start | bytes 688136 | tf_op jit(solution)/shard_map/ppermute | solution.py:266
  54.3 15.2 %all-to-all-start.3 = ((f32[16,1,128]{2,1,0:T(1,128)}), f32[16,1,128]{2,1,0:T(1,128)S(1)}, u32[]{:S(2)}, u32[]{:S(2)}) async-start(f32[16,1,128]{2,1,0:T(1,128)} %moments.3), calls=%async_computation.3 | async-start | bytes 16384 | tf_op jit(solution)/shard_map/all_to_all | solution.py:275
